TPU v7x, 128 devices: a whole 4x4x4 slice. The times are simulated.
128 devices in a mesh: req: 16 (over z, y), kv: 8 (over x, core).
Axes of the slice: x: 4, y: 4, z: 4, core: 2. Of those that a mesh axis runs over, the one named last changes fastest.
Arguments:
- hidden_in: bfloat16 [16384, 2048], P(('req', 'kv')), may hold values from -6 to 6
- slot_tokens: int32 [16384], replicated, may hold values from 0 to 16383, as said below
- cache_len: int32 [128], P('req'), may hold values from 1 to 2048, 65536 in all
- prefill_start: int32 [16], P('req'), may hold values from 0 to 2048
- key_cache: bfloat16 [128, 2048, 1024], P('req', None, 'kv')
- value_cache: bfloat16 [128, 2048, 1024], P('req', None, 'kv'), may hold values from -18 to 18
- key_prefix: bfloat16 [16, 2048, 1024], P('req', None, 'kv')
- value_prefix: bfloat16 [16, 2048, 1024], P('req', None, 'kv'), may hold values from -18 to 18
- attn_gain: float32 [2048], replicated, may hold values from 0.25 to 1.75
- q_proj: bfloat16 [2048, 2048], P(None, 'kv'), may hold values from -0.125 to 0.125
- k_proj: bfloat16 [2048, 1024], P(None, 'kv'), may hold values from -0.125 to 0.125
- v_proj: bfloat16 [2048, 1024], P(None, 'kv'), may hold values from -0.125 to 0.125
- q_gain: float32 [128], replicated, may hold values from 0.25 to 1.75
- k_gain: float32 [128], replicated, may hold values from 0.25 to 1.75
- o_proj: bfloat16 [2048, 2048], P('kv'), may hold values from -0.125 to 0.125
- ffn_gain: float32 [2048], replicated, may hold values from 0.25 to 1.75
- w_gate: bfloat16 [2048, 6144], P(None, 'req'), may hold values from -0.125 to 0.125
- w_up: bfloat16 [2048, 6144], P(None, 'req'), may hold values from -0.125 to 0.125
- w_down: bfloat16 [6144, 2048], P('req'), may hold values from -0.078125 to 0.078125
- final_gain: float32 [2048], replicated, may hold values from 0.25 to 1.75
- lm_head: bfloat16 [2048, 151936], P(None, ('req', 'kv')), may hold values from -0.375 to 0.375
Outputs:
- layer_out: bfloat16 [16384, 2048], P(('req', 'kv'))
- max_logit: float32 [144], replicated
Inputs may be any that keep to these rules, and one draw needn't show every extreme that they name: slot_tokens is a permutation of the batch's tokens; each device's 128 consecutive slots take exactly 1 token from each device's 128 consecutive batch tokens.
All inputs are finite; a program needn't handle non-finite values. No bound on the sum of `cache_len` on one device may be relied on, other than what follows from the above.
Results may differ from a plain program's by a relative error of at most 0.0085.
The roundings to bfloat16 on the way count: a program that leaves them out, or rounds other values in their place, can miss the bound.
Values may be sent and summed in bfloat16 or wider, within the bound.
A program may use at most 128 MiB of HBM per device.

v0:
```python
import jax
import jax.numpy as jnp
from jax import lax
from jax.sharding import PartitionSpec as P

EPS = 1e-06
NEG = -1e30


def spread(value, axis, root):
    mine = lax.axis_index(axis) == root
    return lax.psum(jnp.where(mine, value, jnp.zeros_like(value)), axis)


def norm_rows(values, gain_vec):
    wide = values.astype(jnp.float32)
    return wide * lax.rsqrt(jnp.mean(wide * wide, axis=-1, keepdims=True) + EPS) * gain_vec


def rotate(values, places):
    half_dim = values.shape[-1] // 2
    freqs = 1000000.0 ** (-(jnp.arange(half_dim, dtype=jnp.float32) * 2.0 / values.shape[-1]))
    angles = places[:, None] * freqs[None, :]
    cosine = jnp.cos(angles)[:, None, :]
    sine = jnp.sin(angles)[:, None, :]
    first_half = values[..., :half_dim]
    second_half = values[..., half_dim:]
    return jnp.concatenate(
        [first_half * cosine - second_half * sine, second_half * cosine + first_half * sine],
        axis=-1,
    )


def prefill_full(q_heads, key_old, value_old, key_new, value_new, start_at):
    old_len = key_old.shape[0]
    fresh_rows = q_heads.shape[0]
    factor = q_heads.shape[-1] ** (-0.5)
    all_keys = jnp.concatenate([key_old, key_new], axis=0)
    all_values = jnp.concatenate([value_old, value_new], axis=0)
    scores = (
        jnp.einsum("cgd,kd->gck", q_heads, all_keys, preferred_element_type=jnp.float32) * factor
    )
    key_index = jnp.arange(old_len + fresh_rows, dtype=jnp.int32)[None, :]
    row_index = jnp.arange(fresh_rows, dtype=jnp.int32)[:, None]
    allowed = jnp.where(key_index < old_len, key_index < start_at, key_index - old_len <= row_index)
    scores = jnp.where(allowed[None], scores, NEG)
    row_peak = jnp.max(scores, axis=-1, keepdims=True)
    expd = jnp.exp(scores - row_peak)
    weights = (expd / jnp.sum(expd, axis=-1, keepdims=True)).astype(jnp.bfloat16)
    return jnp.einsum(
        "gck,kd->cgd", weights, all_values, preferred_element_type=jnp.float32
    ).astype(jnp.bfloat16)


def decode_attend(q_heads, key_old, value_old, key_self, value_self, lengths):
    factor = q_heads.shape[-1] ** (-0.5)
    past = jnp.einsum("bgd,bld->bgl", q_heads, key_old, preferred_element_type=jnp.float32) * factor
    slot_index = jnp.arange(key_old.shape[1], dtype=jnp.int32)
    past = jnp.where(slot_index[None, None, :] < lengths[:, None, None], past, NEG)
    own_score = (
        jnp.einsum("bgd,bd->bg", q_heads, key_self, preferred_element_type=jnp.float32) * factor
    )
    row_peak = jnp.maximum(jnp.max(past, axis=-1), own_score)
    past_exp = jnp.exp(past - row_peak[..., None])
    own_exp = jnp.exp(own_score - row_peak)
    row_total = jnp.sum(past_exp, axis=-1) + own_exp
    past_w = (past_exp / row_total[..., None]).astype(jnp.bfloat16)
    own_w = (own_exp / row_total).astype(jnp.bfloat16)
    summed = jnp.einsum("bgl,bld->bgd", past_w, value_old, preferred_element_type=jnp.float32)
    summed = (
        summed + own_w.astype(jnp.float32)[..., None] * value_self.astype(jnp.float32)[:, None, :]
    )
    return summed.astype(jnp.bfloat16)


def regroup(rows_in):
    return lax.all_to_all(rows_in, ("req", "kv"), split_axis=0, concat_axis=0, tiled=True)


def shards(
    hidden_in,
    slot_tokens,
    cache_len,
    prefill_start,
    key_cache,
    value_cache,
    key_prefix,
    value_prefix,
    attn_gain,
    q_proj,
    k_proj,
    v_proj,
    q_gain,
    k_gain,
    o_proj,
    ffn_gain,
    w_gate,
    w_up,
    w_down,
    final_gain,
    lm_head,
):
    req_count = lax.axis_size("req")
    kv_count = lax.axis_size("kv")
    devices = req_count * kv_count
    rows_dev = hidden_in.shape[0]
    per_pair = rows_dev // devices
    self_index = lax.axis_index("req") * kv_count + lax.axis_index("kv")
    slot_table = slot_tokens.reshape(devices, rows_dev)
    from_self = slot_table // rows_dev == self_index
    picked = jnp.argsort(jnp.where(from_self, 0, 1).astype(jnp.int32), axis=1, stable=True)[
        :, :per_pair
    ]
    send_rows = (jnp.take_along_axis(slot_table, picked, axis=1) - self_index * rows_dev).reshape(
        -1
    )
    own_sources = lax.dynamic_index_in_dim(slot_table, self_index, 0, keepdims=False) // rows_dev
    marks = (own_sources[:, None] == jnp.arange(devices, dtype=jnp.int32)[None, :]).astype(
        jnp.int32
    )
    ranks = jnp.sum(marks * (jnp.cumsum(marks, axis=0) - 1), axis=1)
    slot_place = own_sources * per_pair + ranks
    arrived = regroup(hidden_in[send_rows])
    owner_rows = arrived[slot_place]
    normed = norm_rows(owner_rows, attn_gain).astype(jnp.bfloat16)
    q_cols = q_proj.shape[1]
    kv_cols = k_proj.shape[1]
    rows_piece = lax.all_gather(normed, "kv", axis=0, tiled=True)
    projected = jnp.concatenate(
        [
            jnp.dot(rows_piece, q_proj, preferred_element_type=jnp.float32),
            jnp.dot(rows_piece, k_proj, preferred_element_type=jnp.float32),
            jnp.dot(rows_piece, v_proj, preferred_element_type=jnp.float32),
        ],
        axis=1,
    )
    tok_req = projected.shape[0]
    head_dim = q_gain.shape[0]
    dec_count = cache_len.shape[0]
    fresh_count = tok_req - dec_count
    q_raw = projected[:, :q_cols].reshape(tok_req, q_cols // head_dim, head_dim)
    k_raw = projected[:, q_cols : q_cols + kv_cols].reshape(tok_req, kv_cols // head_dim, head_dim)
    v_new = (
        projected[:, q_cols + kv_cols :]
        .astype(jnp.bfloat16)
        .reshape(tok_req, kv_cols // head_dim, head_dim)
    )
    places = jnp.concatenate(
        [prefill_start[0] + jnp.arange(fresh_count, dtype=jnp.int32), cache_len]
    ).astype(jnp.float32)
    queries = rotate(norm_rows(q_raw, q_gain), places).astype(jnp.bfloat16)
    keys_new = rotate(norm_rows(k_raw, k_gain), places).astype(jnp.bfloat16)
    pre_out = prefill_full(
        queries[:fresh_count],
        key_prefix[0, :, 0:head_dim],
        value_prefix[0, :, 0:head_dim],
        keys_new[:fresh_count, 0],
        v_new[:fresh_count, 0],
        prefill_start[0],
    )
    dec_out = decode_attend(
        queries[fresh_count:],
        key_cache,
        value_cache,
        keys_new[fresh_count:, 0],
        v_new[fresh_count:, 0],
        cache_len,
    )
    pieces = jnp.concatenate([pre_out, dec_out], axis=0)
    attended = pieces.reshape(tok_req, q_cols)
    attn_part = lax.psum_scatter(
        jnp.dot(attended, o_proj, preferred_element_type=jnp.float32),
        "kv",
        scatter_dimension=0,
        tiled=True,
    )
    resid = (owner_rows.astype(jnp.float32) + attn_part).astype(jnp.bfloat16)
    ffn_in = norm_rows(resid, ffn_gain).astype(jnp.bfloat16)
    rows_piece = lax.all_gather(ffn_in, "req", axis=0, tiled=True)
    gate_part = jnp.dot(rows_piece, w_gate, preferred_element_type=jnp.float32)
    up_part = jnp.dot(rows_piece, w_up, preferred_element_type=jnp.float32)
    hidden_act = (jax.nn.silu(gate_part) * up_part).astype(jnp.bfloat16)
    ffn_part = lax.psum_scatter(
        jnp.dot(hidden_act, w_down, preferred_element_type=jnp.float32),
        "req",
        scatter_dimension=0,
        tiled=True,
    )
    out_rows = (resid.astype(jnp.float32) + ffn_part).astype(jnp.bfloat16)
    going_back = jnp.zeros_like(out_rows).at[slot_place].set(out_rows)
    returned = regroup(going_back)
    layer_out = jnp.zeros_like(hidden_in).at[send_rows].set(returned)
    tail_rows = norm_rows(out_rows[rows_dev - dec_count - 1 :], final_gain).astype(jnp.bfloat16)
    tail_rows = spread(tail_rows, "kv", kv_count - 1)
    local_peaks = jnp.max(
        jnp.dot(
            lax.all_gather(tail_rows, "req", axis=0, tiled=True),
            lm_head,
            preferred_element_type=jnp.float32,
        ),
        axis=1,
    )
    max_logit = lax.pmax(local_peaks, ("req", "kv"))
    return (layer_out, max_logit)


def solution(mesh):
    placed = (
        P(("req", "kv"), None),
        P(),
        P("req"),
        P("req"),
        P("req", None, "kv"),
        P("req", None, "kv"),
        P("req", None, "kv"),
        P("req", None, "kv"),
        P(),
        P(None, "kv"),
        P(None, "kv"),
        P(None, "kv"),
        P(),
        P(),
        P("kv", None),
        P(),
        P(None, "req"),
        P(None, "req"),
        P("req", None),
        P(),
        P(None, ("req", "kv")),
    )
    return jax.shard_map(
        shards, mesh=mesh, in_specs=placed, out_specs=(P(("req", "kv"), None), P()), check_vma=False
    )
```

profile of v0, /device:TPU:1, one launch (start us, length us, event | category | flops | bytes accessed | tf_op | source)
XLA Modules:
  0.0 540.3 jit_solution(2482450521483599496)
XLA Ops:
  7.2 1.7 fusion.60
  11.1 4.7 sort.19.cloned.1.call-done
  17.0 1.9 gather_fusion.2
  23.6 11.5 %all-to-all-start = ((bf16[128,2,1024]{2,1,0:T(2,128)(2,1)}), bf16[128,2,1024]{2,1,0:T(2,128)(2,1)S(1)}, u32[]{:S(2)}, u32[]{:S(2)}) async-start(bf16[128,2,1024]{2,1,0:T(2,128)(2,1)} %reshape.484), calls=%async_computation | async-start | bytes 1048576 | tf_op jit(solution)/shard_map/all_to_all | solution.py:77
  35.9 13.0 %all-to-all-done = bf16[128,2,1024]{2,1,0:T(2,128)(2,1)S(1)} async-done(((bf16[128,2,1024]{2,1,0:T(2,128)(2,1)}), bf16[128,2,1024]{2,1,0:T(2,128)(2,1)S(1)}, u32[]{:S(2)}, u32[]{:S(2)}) %all-to-all-start) | async-done | bytes 524320 | tf_op jit(solution)/shard_map/all_to_all | solution.py:77
  48.9 1.7 reshape.485
  50.6 1.5 copy.105
  55.4 3.1 multiply_cosine_fusion
  58.6 4.2 fusion.4
  62.7 20.4 %all-gather.4.cloned.1.call-done = bf16[1024,2048]{1,0:T(8,128)(2,1)} async-done(((bf16[128,2048]{1,0:T(8,128)(2,1)}), bf16[1024,2048]{1,0:T(8,128)(2,1)}) %all-gather.4.cloned.1.call-update) | async-done | bytes 4194320 | tf_op jit(solution)/shard_map/all_gather | solution.py:128
  83.2 3.6 convolution_convert_fusion
  87.5 1.5 multiply_reduce_fusion.1
  90.5 2.3 multiply_reduce_fusion
  92.8 1.5 copy.81
  95.7 1.8 subtract_convert_fusion
  99.4 2.9 fusion.43
  102.4 15.9 %fusion.84 = (f32[2,1016]{1,0:T(2,128)S(1)}, f32[2,1016,3064]{2,1,0:T(8,128)}) fusion(pred[1016,3064]{1,0:T(8,128)(4,1)} %fusion.4, bf16[1016,128]{1,0:T(8,128)(2,1)} %copy.80, bf16[2048,128]{1,0:T(8,128)(2,1)} %bitcast.105, bf16[1024,2,64]{2,0,1:T(8,128)(2,1)S(1)} %get-tuple-element.6, bf16[1024,2,64]{2,0,1:T(8,128)(2,1)S(1)} %get-tuple-element.7), kind=kOutput, calls=%fused_computation.161 | convolution fusion | flops 1621384704 | bytes 29334016 | tf_op jit(solution)/shard_map/sub | solution.py:48
  118.3 11.7 %fusion.12 = bf16[1016,2,128]{2,0,1:T(8,128)(2,1)S(1)} fusion(f32[2,1016,3064]{2,1,0:T(8,128)} %get-tuple-element.21, f32[2,1016]{1,0:T(2,128)S(1)} %get-tuple-element.20, bf16[1016,128]{1,0:T(8,128)(2,1)S(1)} %copy-done.5, bf16[2048,128]{1,0:T(8,128)(2,1)} %bitcast.106), kind=kOutput, calls=%fused_computation.28 | convolution fusion | flops 1608149248 | bytes 26216896 | tf_op jit(solution)/shard_map/gck,kd->cgd/dot_general | solution.py:50
  130.3 5.7 %fusion.89 = f32[1024,2048]{1,0:T(8,128)} fusion(bf16[1024,256]{0,1:T(8,128)(2,1)S(1)} %bitcast.94, bf16[256,2048]{1,0:T(8,128)(2,1)} %param.35), kind=kOutput, calls=%fused_computation.162 | convolution fusion | flops 1073741824 | bytes 9961472 | tf_op jit(solution)/shard_map/dot_general | solution.py:172
  136.1 51.5 %reduce-scatter.3.cloned.1.call-done = f32[128,2048]{1,0:T(8,128)} async-done(((f32[1024,2048]{1,0:T(8,128)}), f32[128,2048]{1,0:T(8,128)}) %reduce-scatter.3.cloned.1.call-update) | async-done | bytes 1048592 | tf_op jit(solution)/shard_map/reduce_scatter | solution.py:171
  187.7 1.5 fusion.17
  190.4 71.2 %all-gather.6.cloned.1.call-done = bf16[2048,2048]{1,0:T(8,128)(2,1)} async-done(((bf16[128,2048]{1,0:T(8,128)(2,1)}), bf16[2048,2048]{1,0:T(8,128)(2,1)}) %all-gather.6.cloned.1.call-update) | async-done | bytes 8388624 | tf_op jit(solution)/shard_map/all_gather | solution.py:179
  261.5 10.1 %fusion.90 = f32[2048,384]{1,0:T(8,128)} fusion(bf16[2048,2048]{1,0:T(8,128)(2,1)} %all-gather.6.cloned.1.call-done, bf16[2048,384]{1,0:T(8,128)(2,1)} %param.37), kind=kOutput, calls=%fused_computation.163 | convolution fusion | flops 3221225472 | bytes 13107200 | tf_op jit(solution)/shard_map/dot_general | solution.py:180
  271.6 15.4 %fusion.10 = f32[2048,2048]{1,0:T(8,128)} fusion(bf16[384,2048]{1,0:T(8,128)(2,1)S(1)} %copy-done, f32[2048,384]{1,0:T(8,128)} %fusion.90, bf16[2048,2048]{1,0:T(8,128)(2,1)} %all-gather.6.cloned.1.call-done, bf16[2048,384]{1,0:T(8,128)(2,1)} %param.38), kind=kOutput, calls=%fused_computation.26 | convolution fusion | flops 6447169536 | bytes 31457280 | tf_op jit(solution)/shard_map/dot_general | solution.py:184
  287.0 110.1 %reduce-scatter.5.cloned.1.call-done = f32[128,2048]{1,0:T(8,128)} async-done(((f32[2048,2048]{1,0:T(8,128)}), f32[128,2048]{1,0:T(8,128)}) %reduce-scatter.5.cloned.1.call-update) | async-done | bytes 1048592 | tf_op jit(solution)/shard_map/reduce_scatter | solution.py:183
  398.6 1.5 scatter_custom_fusion
  402.4 23.1 %psum.7 = bf16[9,2048]{1,0:T(8,128)(2,1)S(1)} all-reduce(bf16[9,2048]{1,0:T(8,128)(2,1)S(1)} %fusion.48), channel_id=1, replica_groups=mesh['req'=16,'kv'=8] {'kv'}, use_global_device_ids=true, to_apply=%region_16.17 | all-reduce | flops 18432 | bytes 73728 | tf_op jit(solution)/shard_map/psum | solution.py:12
  425.5 8.6 %all-to-all-start.1 = ((bf16[128,2,1024]{2,1,0:T(2,128)(2,1)}), bf16[128,2,1024]{2,1,0:T(2,128)(2,1)S(1)}, u32[]{:S(2)}, u32[]{:S(2)}) async-start(bf16[128,2,1024]{2,1,0:T(2,128)(2,1)} %reshape.486), calls=%async_computation.3 | async-start | bytes 1048576 | tf_op jit(solution)/shard_map/all_to_all | solution.py:77
  434.1 22.4 %all-gather = bf16[16,9,2048]{2,1,0:T(8,128)(2,1)S(1)} all-gather(bf16[1,9,2048]{2,1,0:T(8,128)(2,1)S(1)} %bitcast.99), channel_id=1, replica_groups=mesh['req'=16,'kv'=8] {'req'}, dimensions={0}, use_global_device_ids=true | all-gather | bytes 626688 | tf_op jit(solution)/shard_map/all_gather | solution.py:197
  457.5 4.4 convolution_reduce_fusion
  461.9 68.8 %pmax.7 = f32[144]{0:T(256)} all-reduce(f32[144]{0:T(256)S(1)} %convolution_reduce_fusion), channel_id=1, replica_groups=mesh['req'=16,'kv'=8] {'req','kv'}, use_global_device_ids=true, to_apply=%region_18.19 | all-reduce | flops 144 | bytes 1152 | tf_op jit(solution)/shard_map/pmax | solution.py:203
  531.1 2.4 scatter_custom_fusion.1
  (102 shorter events, 23.8 us)
Async XLA Ops:
  7.2 264.4 %copy-start = (bf16[384,2048]{1,0:T(8,128)(2,1)S(1)}, bf16[384,2048]{1,0:T(8,128)(2,1)}, u32[]{:S(2)}) copy-start(bf16[384,2048]{1,0:T(8,128)(2,1)} %param.39) | copy-start | bytes 4718596
  7.2 12.8 %copy-start.1 = (bf16[128,2048]{1,0:T(8,128)(2,1)S(1)}, bf16[128,2048]{1,0:T(8,128)(2,1)}, u32[]{:S(2)}) copy-start(bf16[128,2048]{1,0:T(8,128)(2,1)} %param.21) | copy-start | bytes 1572868
  7.2 8.5 %sort.19.cloned.1.call-start = ((), (), s32[]{:S(2)}) async-start(), calls=%async_computation.8 | async-start | bytes 393248 | tf_op jit(solution)/shard_map/jit(argsort)/sort | solution.py:111
  23.6 25.2 %all-to-all-start = ((bf16[128,2,1024]{2,1,0:T(2,128)(2,1)}), bf16[128,2,1024]{2,1,0:T(2,128)(2,1)S(1)}, u32[]{:S(2)}, u32[]{:S(2)}) async-start(bf16[128,2,1024]{2,1,0:T(2,128)(2,1)} %reshape.484), calls=%async_computation | async-start | bytes 1048576 | tf_op jit(solution)/shard_map/all_to_all | solution.py:77
  35.1 48.0 %all-gather.4.cloned.1.call-start = ((), (), s32[]{:S(2)}) async-start(), calls=%async_computation.4 | async-start | bytes 4718592 | tf_op jit(solution)/shard_map/all_gather | solution.py:128
  35.9 17.4 %copy-start.6 = (f32[2048]{0:T(1024)S(1)}, f32[2048]{0:T(1024)}, u32[]{:S(2)}) copy-start(f32[2048]{0:T(1024)} %param.29) | copy-start | bytes 24580
  50.6 4.7 copy-start.9
  53.1 30.1 %copy-start.13 = (bf16[2048,128]{1,0:T(8,128)(2,1)S(1)}, bf16[2048,128]{1,0:T(8,128)(2,1)}, u32[]{:S(2)}) copy-start(bf16[2048,128]{1,0:T(8,128)(2,1)} %param.32) | copy-start | bytes 1572868
  54.3 133.4 %reduce-scatter.3.cloned.1.call-start = ((), (), s32[]{:S(2)}) async-start(), calls=%async_computation.5 | async-start | bytes 9437184 | tf_op jit(solution)/shard_map/reduce_scatter | solution.py:171
  62.7 24.8 %copy-start.4 = (bf16[2048,128]{1,0:T(8,128)(2,1)S(1)}, bf16[2048,128]{1,0:T(8,128)(2,1)}, u32[]{:S(2)}) copy-start(bf16[2048,128]{1,0:T(8,128)(2,1)} %param.31) | copy-start | bytes 1572868
  83.2 4.4 copy-start.3
  86.8 2.3 copy-start.10
  86.8 3.7 copy-start.12
  90.5 4.8 copy-start.11
  95.3 2.5 copy-start.2
  102.4 15.9 %copy-start.5 = (bf16[1016,128]{1,0:T(8,128)(2,1)S(1)}, bf16[1016,128]{1,0:T(8,128)(2,1)}, u32[]{:S(2)}) copy-start(bf16[1016,128]{1,0:T(8,128)(2,1)} %slice.58) | copy-start | bytes 780292
  136.1 53.1 %copy-start.7 = (f32[2048]{0:T(1024)S(1)}, f32[2048]{0:T(1024)}, u32[]{:S(2)}) copy-start(f32[2048]{0:T(1024)} %param.36) | copy-start | bytes 24580
  136.1 125.4 %all-gather.6.cloned.1.call-start = ((), (), s32[]{:S(2)}) async-start(), calls=%async_computation.6 | async-start | bytes 8912896 | tf_op jit(solution)/shard_map/all_gather | solution.py:179
  190.1 207.0 %reduce-scatter.5.cloned.1.call-start = ((), (), s32[]{:S(2)}) async-start(), calls=%async_computation.7 | async-start | bytes 17825792 | tf_op jit(solution)/shard_map/reduce_scatter | solution.py:183
  287.0 115.3 %copy-start.8 = (f32[2048]{0:T(1024)S(1)}, f32[2048]{0:T(1024)}, u32[]{:S(2)}) copy-start(f32[2048]{0:T(1024)} %param.40) | copy-start | bytes 24580
  425.5 105.2 %all-to-all-start.1 = ((bf16[128,2,1024]{2,1,0:T(2,128)(2,1)}), bf16[128,2,1024]{2,1,0:T(2,128)(2,1)S(1)}, u32[]{:S(2)}, u32[]{:S(2)}) async-start(bf16[128,2,1024]{2,1,0:T(2,128)(2,1)} %reshape.486), calls=%async_computation.3 | async-start | bytes 1048576 | tf_op jit(solution)/shard_map/all_to_all | solution.py:77
Sparse Core Ops, SparseCore 0:
  10.8 4.6 sort.21.cloned.1.call-done
  54.4 28.7 all-gather.3
  136.2 51.3 reduce-scatter.2
  190.4 71.0 all-gather.5
  287.1 109.9 reduce-scatter.4
  (1 shorter events, 0.0 us)
where the time goes:
time: 545 us; the launch traced here: 540 us
  waiting for transfers between devices  266 us (49%)
  blocking collectives  114 us (21%)
  matrix products  74.9 us (14%)
  local copies, waits for them, and re-layouts  25.5 us (5%)
  other arithmetic  23.6 us (4%)
  starting transfers between devices  20.7 us (4%)
  between operations  15 us (3%)
    reduce_scatter x1, waiting for transfers between devices, shards(): lax.psum_scatter(jnp.dot(hidden_act, w_down, preferred_element_type=jnp.f...  110 us
    all_gather x1, waiting for transfers between devices, shards(): rows_piece = lax.all_gather(ffn_in, 'req', axis=0, tiled=True)  71.2 us
    pmax x1, blocking collectives, shards(): max_logit = lax.pmax(local_peaks, ('req', 'kv'))  68.8 us
    reduce_scatter x1, waiting for transfers between devices, shards(): lax.psum_scatter(jnp.dot(attended, o_proj, preferred_element_type=jnp.flo...  51.5 us
    psum x1, blocking collectives, spread(): return lax.psum(jnp.where(mine, value, jnp.zeros_like(value)), axis)  23.1 us
    all_gather x1, blocking collectives, shards(): lax.all_gather(tail_rows, 'req', axis=0, tiled=True)  22.4 us
    all_gather x1, waiting for transfers between devices, shards(): rows_piece = lax.all_gather(normed, 'kv', axis=0, tiled=True)  20.4 us
    all_to_all x2, starting transfers between devices, regroup(): lax.all_to_all(rows_in, ('req', 'kv'), split_axis=0, concat_axis=0, tiled...  20.1 us
  transfers between devices with their start and end apart: 6, of which 5 were waited for; matrix products, arithmetic and copies ran while one was open for 3% of the time, Pallas kernels for 0%

commit v1 on v0

--- a/solution.py
+++ b/solution.py
@@ -176,7 +176,11 @@
     )
     resid = (owner_rows.astype(jnp.float32) + attn_part).astype(jnp.bfloat16)
     ffn_in = norm_rows(resid, ffn_gain).astype(jnp.bfloat16)
-    rows_piece = lax.all_gather(ffn_in, "req", axis=0, tiled=True)
+    peers = lax.axis_size("req")
+    repeats = [peers if d == 0 else 1 for d in range(ffn_in.ndim)]
+    rows_piece = lax.all_to_all(
+        jnp.tile(ffn_in, repeats), "req", split_axis=0, concat_axis=0, tiled=True
+    )
     gate_part = jnp.dot(rows_piece, w_gate, preferred_element_type=jnp.float32)
     up_part = jnp.dot(rows_piece, w_up, preferred_element_type=jnp.float32)
     hidden_act = (jax.nn.silu(gate_part) * up_part).astype(jnp.bfloat16)

time: 545 us -> 574 us (1.053)
  blocking collectives: 114 us -> 216 us
  waiting for transfers between devices: 266 us -> 194 us
    all_to_all x0 -> x1, blocking collectives: none -> 102 us  [shards(): lax.all_to_all(jnp.tile(ffn_in, repeats), 'req', split_axis=0, concat_axi...]
    all_gather x1 -> x0, waiting for transfers between devices: 71.2 us -> none  [shards(): rows_piece = lax.all_gather(ffn_in, 'req', axis=0, tiled=True)]
  transfers between devices with their start and end apart: 6 -> 5, of which waited for: 5 -> 4; matrix products, arithmetic and copies ran while one was open for 3% -> 2% of each run, Pallas kernels for 0% -> 0%
where the time goes in v1:
time: 574 us; the launch traced here: 570 us
  blocking collectives  216 us (38%)
  waiting for transfers between devices  194 us (34%)
  matrix products  70.9 us (12%)
  local copies, waits for them, and re-layouts  29.8 us (5%)
  other arithmetic  22.8 us (4%)
  starting transfers between devices  20.7 us (4%)
  between operations  15.1 us (3%)
    reduce_scatter x1, waiting for transfers between devices, shards(): lax.psum_scatter(jnp.dot(hidden_act, w_down, preferred_element_type=jnp.f...  109 us
    all_to_all x1, blocking collectives, shards(): lax.all_to_all(jnp.tile(ffn_in, repeats), 'req', split_axis=0, concat_axi...  102 us
    pmax x1, blocking collectives, shards(): max_logit = lax.pmax(local_peaks, ('req', 'kv'))  68.8 us
    reduce_scatter x1, waiting for transfers between devices, shards(): lax.psum_scatter(jnp.dot(attended, o_proj, preferred_element_type=jnp.flo...  51.5 us
    psum x1, blocking collectives, spread(): return lax.psum(jnp.where(mine, value, jnp.zeros_like(value)), axis)  23.1 us
    all_gather x1, blocking collectives, shards(): lax.all_gather(tail_rows, 'req', axis=0, tiled=True)  22.4 us
    all_gather x1, waiting for transfers between devices, shards(): rows_piece = lax.all_gather(normed, 'kv', axis=0, tiled=True)  20.2 us
    all_to_all x2, starting transfers between devices, regroup(): lax.all_to_all(rows_in, ('req', 'kv'), split_axis=0, concat_axis=0, tiled...  20.1 us
  transfers between devices with their start and end apart: 5, of which 4 were waited for; matrix products, arithmetic and copies ran while one was open for 2% of the time, Pallas kernels for 0%

profile of v1, /device:TPU:1, one launch (start us, length us, event | category | flops | bytes accessed | tf_op | source)
XLA Modules:
  0.0 569.6 jit_solution(646262338270673463)
XLA Ops:
  7.2 1.7 fusion.60
  11.1 4.7 sort.19.cloned.1.call-done
  17.0 1.9 gather_fusion.2
  23.6 11.5 %all-to-all-start = ((bf16[128,2,1024]{2,1,0:T(2,128)(2,1)}), bf16[128,2,1024]{2,1,0:T(2,128)(2,1)S(1)}, u32[]{:S(2)}, u32[]{:S(2)}) async-start(bf16[128,2,1024]{2,1,0:T(2,128)(2,1)} %reshape.491), calls=%async_computation | async-start | bytes 1048576 | tf_op jit(solution)/shard_map/all_to_all | solution.py:77
  35.9 13.0 %all-to-all-done = bf16[128,2,1024]{2,1,0:T(2,128)(2,1)S(1)} async-done(((bf16[128,2,1024]{2,1,0:T(2,128)(2,1)}), bf16[128,2,1024]{2,1,0:T(2,128)(2,1)S(1)}, u32[]{:S(2)}, u32[]{:S(2)}) %all-to-all-start) | async-done | bytes 524320 | tf_op jit(solution)/shard_map/all_to_all | solution.py:77
  48.9 1.7 reshape.492
  50.6 1.5 copy.105
  55.6 3.1 multiply_cosine_fusion
  58.8 4.2 fusion.4
  63.0 20.2 %all-gather.3.cloned.1.call-done = bf16[1024,2048]{1,0:T(8,128)(2,1)} async-done(((bf16[128,2048]{1,0:T(8,128)(2,1)}), bf16[1024,2048]{1,0:T(8,128)(2,1)}) %all-gather.3.cloned.1.call-update) | async-done | bytes 4194320 | tf_op jit(solution)/shard_map/all_gather | solution.py:128
  83.2 3.6 convolution_convert_fusion
  87.5 1.5 multiply_reduce_fusion.1
  90.5 2.3 multiply_reduce_fusion
  92.8 1.5 copy.81
  95.7 1.8 subtract_convert_fusion
  99.5 2.9 fusion.43
  102.4 15.5 %fusion.84 = (f32[2,1016]{1,0:T(2,128)S(1)}, f32[2,1016,3064]{2,1,0:T(8,128)}) fusion(pred[1016,3064]{1,0:T(8,128)(4,1)} %fusion.4, bf16[1016,128]{1,0:T(8,128)(2,1)} %copy.80, bf16[2048,128]{1,0:T(8,128)(2,1)} %bitcast.108, bf16[1024,2,64]{2,0,1:T(8,128)(2,1)S(1)} %get-tuple-element.6, bf16[1024,2,64]{2,0,1:T(8,128)(2,1)S(1)} %get-tuple-element.7), kind=kOutput, calls=%fused_computation.161 | convolution fusion | flops 1621384704 | bytes 29334016 | tf_op jit(solution)/shard_map/sub | solution.py:48
  118.0 11.7 %fusion.12 = bf16[1016,2,128]{2,0,1:T(8,128)(2,1)S(1)} fusion(f32[2,1016,3064]{2,1,0:T(8,128)} %get-tuple-element.21, f32[2,1016]{1,0:T(2,128)S(1)} %get-tuple-element.20, bf16[1016,128]{1,0:T(8,128)(2,1)S(1)} %copy-done.6, bf16[2048,128]{1,0:T(8,128)(2,1)} %bitcast.109), kind=kOutput, calls=%fused_computation.28 | convolution fusion | flops 1608149248 | bytes 26216896 | tf_op jit(solution)/shard_map/gck,kd->cgd/dot_general | solution.py:50
  130.0 5.7 %fusion.89 = f32[1024,2048]{1,0:T(8,128)} fusion(bf16[1024,256]{0,1:T(8,128)(2,1)S(1)} %bitcast.97, bf16[256,2048]{1,0:T(8,128)(2,1)} %param.35), kind=kOutput, calls=%fused_computation.162 | convolution fusion | flops 1073741824 | bytes 9961472 | tf_op jit(solution)/shard_map/dot_general | solution.py:172
  135.8 51.5 %reduce-scatter.3.cloned.1.call-done = f32[128,2048]{1,0:T(8,128)} async-done(((f32[1024,2048]{1,0:T(8,128)}), f32[128,2048]{1,0:T(8,128)}) %reduce-scatter.3.cloned.1.call-update) | async-done | bytes 1048592 | tf_op jit(solution)/shard_map/reduce_scatter | solution.py:171
  190.0 101.9 %all_to_all.33 = bf16[16,128,2048]{2,1,0:T(8,128)(2,1)S(1)} all-to-all(bf16[16,128,2048]{2,1,0:T(8,128)(2,1)S(1)} %tile.2), channel_id=1, replica_groups=mesh['req'=16,'kv'=8] {'req'}, dimensions={0} | all-to-all | bytes 16777216 | tf_op jit(solution)/shard_map/all_to_all | solution.py:181
  291.9 3.2 copy-done.2
  295.1 6.4 %fusion.90 = f32[2048,384]{1,0:T(8,128)} fusion(bf16[2048,2048]{1,0:T(8,128)(2,1)S(1)} %bitcast.92, bf16[2048,384]{1,0:T(8,128)(2,1)S(1)} %copy-done.13), kind=kOutput, calls=%fused_computation.163 | convolution fusion | flops 3221225472 | bytes 13107200 | tf_op jit(solution)/shard_map/dot_general | solution.py:184
  301.6 15.4 %fusion.10 = f32[2048,2048]{1,0:T(8,128)} fusion(bf16[384,2048]{1,0:T(8,128)(2,1)S(1)} %copy-done, f32[2048,384]{1,0:T(8,128)} %fusion.90, bf16[2048,2048]{1,0:T(8,128)(2,1)} %bitcast.93, bf16[2048,384]{1,0:T(8,128)(2,1)} %param.38), kind=kOutput, calls=%fused_computation.26 | convolution fusion | flops 6447169536 | bytes 31457280 | tf_op jit(solution)/shard_map/dot_general | solution.py:188
  317.0 109.3 %reduce-scatter.5.cloned.1.call-done = f32[128,2048]{1,0:T(8,128)} async-done(((f32[2048,2048]{1,0:T(8,128)}), f32[128,2048]{1,0:T(8,128)}) %reduce-scatter.5.cloned.1.call-update) | async-done | bytes 1048592 | tf_op jit(solution)/shard_map/reduce_scatter | solution.py:187
  427.8 1.5 scatter_custom_fusion
  431.6 23.1 %psum.7 = bf16[9,2048]{1,0:T(8,128)(2,1)S(1)} all-reduce(bf16[9,2048]{1,0:T(8,128)(2,1)S(1)} %fusion.48), channel_id=1, replica_groups=mesh['req'=16,'kv'=8] {'kv'}, use_global_device_ids=true, to_apply=%region_16.17 | all-reduce | flops 18432 | bytes 73728 | tf_op jit(solution)/shard_map/psum | solution.py:12
  454.7 8.6 %all-to-all-start.2 = ((bf16[128,2,1024]{2,1,0:T(2,128)(2,1)}), bf16[128,2,1024]{2,1,0:T(2,128)(2,1)S(1)}, u32[]{:S(2)}, u32[]{:S(2)}) async-start(bf16[128,2,1024]{2,1,0:T(2,128)(2,1)} %reshape.493), calls=%async_computation.4 | async-start | bytes 1048576 | tf_op jit(solution)/shard_map/all_to_all | solution.py:77
  463.3 22.4 %all-gather = bf16[16,9,2048]{2,1,0:T(8,128)(2,1)S(1)} all-gather(bf16[1,9,2048]{2,1,0:T(8,128)(2,1)S(1)} %bitcast.102), channel_id=1, replica_groups=mesh['req'=16,'kv'=8] {'req'}, dimensions={0}, use_global_device_ids=true | all-gather | bytes 626688 | tf_op jit(solution)/shard_map/all_gather | solution.py:201
  486.7 4.4 convolution_reduce_fusion
  491.1 68.8 %pmax.7 = f32[144]{0:T(256)} all-reduce(f32[144]{0:T(256)S(1)} %convolution_reduce_fusion), channel_id=1, replica_groups=mesh['req'=16,'kv'=8] {'req','kv'}, use_global_device_ids=true, to_apply=%region_18.19 | all-reduce | flops 144 | bytes 1152 | tf_op jit(solution)/shard_map/pmax | solution.py:207
  560.4 2.4 scatter_custom_fusion.1
  (105 shorter events, 25.5 us)
Async XLA Ops:
  7.2 294.4 %copy-start = (bf16[384,2048]{1,0:T(8,128)(2,1)S(1)}, bf16[384,2048]{1,0:T(8,128)(2,1)}, u32[]{:S(2)}) copy-start(bf16[384,2048]{1,0:T(8,128)(2,1)} %param.39) | copy-start | bytes 4718596
  7.2 12.8 %copy-start.1 = (bf16[128,2048]{1,0:T(8,128)(2,1)S(1)}, bf16[128,2048]{1,0:T(8,128)(2,1)}, u32[]{:S(2)}) copy-start(bf16[128,2048]{1,0:T(8,128)(2,1)} %param.21) | copy-start | bytes 1572868
  7.2 8.5 %sort.19.cloned.1.call-start = ((), (), s32[]{:S(2)}) async-start(), calls=%async_computation.8 | async-start | bytes 393248 | tf_op jit(solution)/shard_map/jit(argsort)/sort | solution.py:111
  23.6 25.2 %all-to-all-start = ((bf16[128,2,1024]{2,1,0:T(2,128)(2,1)}), bf16[128,2,1024]{2,1,0:T(2,128)(2,1)S(1)}, u32[]{:S(2)}, u32[]{:S(2)}) async-start(bf16[128,2,1024]{2,1,0:T(2,128)(2,1)} %reshape.491), calls=%async_computation | async-start | bytes 1048576 | tf_op jit(solution)/shard_map/all_to_all | solution.py:77
  35.1 48.0 %all-gather.3.cloned.1.call-start = ((), (), s32[]{:S(2)}) async-start(), calls=%async_computation.5 | async-start | bytes 4718592 | tf_op jit(solution)/shard_map/all_gather | solution.py:128
  35.9 17.4 %copy-start.7 = (f32[2048]{0:T(1024)S(1)}, f32[2048]{0:T(1024)}, u32[]{:S(2)}) copy-start(f32[2048]{0:T(1024)} %param.29) | copy-start | bytes 24580
  50.6 5.0 copy-start.10
  53.1 30.1 %copy-start.15 = (bf16[2048,128]{1,0:T(8,128)(2,1)S(1)}, bf16[2048,128]{1,0:T(8,128)(2,1)}, u32[]{:S(2)}) copy-start(bf16[2048,128]{1,0:T(8,128)(2,1)} %param.32) | copy-start | bytes 1572868
  54.3 133.0 %reduce-scatter.3.cloned.1.call-start = ((), (), s32[]{:S(2)}) async-start(), calls=%async_computation.6 | async-start | bytes 9437184 | tf_op jit(solution)/shard_map/reduce_scatter | solution.py:171
  63.0 24.6 %copy-start.5 = (bf16[2048,128]{1,0:T(8,128)(2,1)S(1)}, bf16[2048,128]{1,0:T(8,128)(2,1)}, u32[]{:S(2)}) copy-start(bf16[2048,128]{1,0:T(8,128)(2,1)} %param.31) | copy-start | bytes 1572868
  83.2 4.4 copy-start.4
  86.8 2.3 copy-start.11
  86.8 3.7 copy-start.14
  90.5 4.8 copy-start.12
  95.3 2.5 copy-start.3
  102.4 15.5 %copy-start.6 = (bf16[1016,128]{1,0:T(8,128)(2,1)S(1)}, bf16[1016,128]{1,0:T(8,128)(2,1)}, u32[]{:S(2)}) copy-start(bf16[1016,128]{1,0:T(8,128)(2,1)} %slice.58) | copy-start | bytes 780292
  135.7 53.0 %copy-start.8 = (f32[2048]{0:T(1024)S(1)}, f32[2048]{0:T(1024)}, u32[]{:S(2)}) copy-start(f32[2048]{0:T(1024)} %param.36) | copy-start | bytes 24580
  135.7 290.6 %reduce-scatter.5.cloned.1.call-start = ((), (), s32[]{:S(2)}) async-start(), calls=%async_computation.7 | async-start | bytes 17825792 | tf_op jit(solution)/shard_map/reduce_scatter | solution.py:187
  190.0 105.1 %copy-start.13 = (bf16[2048,384]{1,0:T(8,128)(2,1)S(1)}, bf16[2048,384]{1,0:T(8,128)(2,1)}, u32[]{:S(2)}) copy-start(bf16[2048,384]{1,0:T(8,128)(2,1)} %param.37) | copy-start | bytes 4718596
  291.9 3.2 copy-start.2
  317.0 114.5 %copy-start.9 = (f32[2048]{0:T(1024)S(1)}, f32[2048]{0:T(1024)}, u32[]{:S(2)}) copy-start(f32[2048]{0:T(1024)} %param.40) | copy-start | bytes 24580
  454.7 105.2 %all-to-all-start.2 = ((bf16[128,2,1024]{2,1,0:T(2,128)(2,1)}), bf16[128,2,1024]{2,1,0:T(2,128)(2,1)S(1)}, u32[]{:S(2)}, u32[]{:S(2)}) async-start(bf16[128,2,1024]{2,1,0:T(2,128)(2,1)} %reshape.493), calls=%async_computation.4 | async-start | bytes 1048576 | tf_op jit(solution)/shard_map/all_to_all | solution.py:77
Sparse Core Ops, SparseCore 0:
  10.8 4.6 sort.21.cloned.1.call-done
  54.4 28.7 all-gather.2
  135.9 51.3 reduce-scatter.2
  317.1 109.1 reduce-scatter.4
  (1 shorter events, 0.0 us)
